TPU v7x, 256 devices: a whole 4x4x8 slice. The times are simulated.
256 devices in a mesh: dp: 8 (over y, core), ctx: 32 (over z, x).
Axes of the slice: x: 4, y: 4, z: 8, core: 2. Of those that a mesh axis runs over, the one named last changes fastest.
Arguments:
- normed_hidden_input: bfloat16 [8, 4096, 4096], P('dp', 'ctx'), may hold values from -6 to 6
- frozen_query_projection: bfloat16 [8, 4096, 4096], P('dp', 'ctx'), may hold values from -24 to 24
- frozen_key_projection: bfloat16 [8, 4096, 4096], P('dp', 'ctx'), may hold values from -24 to 24
- frozen_value_projection: bfloat16 [8, 4096, 4096], P('dp', 'ctx'), may hold values from -6 to 6
- cotangent: bfloat16 [8, 4096, 4096], P('dp', 'ctx'), may hold values from -0.119628906 to 0.119628906
- adapter_down_maps: bfloat16 [3, 4096, 16], replicated, may hold values from -0.09375 to 0.09375
- adapter_up_maps: bfloat16 [3, 16, 4096], replicated, may hold values from -1.5 to 1.5
- head_shift_mask: int32 [32], replicated, may hold values from 0 to 1, as said below
Outputs:
- context: bfloat16 [8, 4096, 4096], P('dp', 'ctx')
- grad_down: float32 [3, 4096, 16], replicated
- grad_up: float32 [3, 16, 4096], replicated
Inputs may be any that keep to these rules, and one draw needn't show every extreme that they name: `head_shift_mask`: exactly half of the entries are 1, the rest 0; which heads are shifted varies.
All inputs are finite; a program needn't handle non-finite values.
Results may differ from a plain program's by a relative error of at most 0.02.
The roundings to bfloat16 on the way count: a program that leaves them out, or rounds other values in their place, can miss the bound.
Values may be sent and summed in bfloat16 or wider, within the bound.
A program may use at most 64 MiB of HBM per device.

v0:
```python
import math
import jax
import jax.numpy as jnp
from jax import lax
from jax.sharding import PartitionSpec as P

HEAD_DIM = 128
GROUP = 1024
SHIFT = 512
adapter_scale = 0.25


def shift_heads(values, shift_flags, amount):
    rolled = jnp.roll(values, amount, axis=0)
    return jnp.where(shift_flags[None, :, None] == 1, rolled, values)


def group_block(segment_list):
    queries, key_rows, value_rows, grad_out = segment_list
    group_len = queries.shape[0]
    softmax_scale = 1.0 / math.sqrt(queries.shape[2])
    scores = (
        jnp.einsum("qhe,khe->hqk", queries, key_rows, preferred_element_type=jnp.float32)
        * softmax_scale
    )
    row_ids = lax.broadcasted_iota(jnp.int32, (group_len, group_len), 0)
    col_ids = lax.broadcasted_iota(jnp.int32, (group_len, group_len), 1)
    scores = jnp.where((col_ids <= row_ids)[None], scores, -1e30)
    highest = jnp.max(scores, axis=2, keepdims=True)
    exponent = jnp.exp(scores - highest)
    weights = exponent / jnp.sum(exponent, axis=2, keepdims=True)
    weights_low = weights.astype(jnp.bfloat16)
    attended = jnp.einsum(
        "hqk,khe->qhe", weights_low, value_rows, preferred_element_type=jnp.float32
    ).astype(jnp.bfloat16)
    weight_grad = jnp.einsum(
        "qhe,khe->hqk", grad_out, value_rows, preferred_element_type=jnp.float32
    )
    row_inner = jnp.sum(grad_out.astype(jnp.float32) * attended.astype(jnp.float32), axis=2)
    score_grad = weights * (weight_grad - jnp.transpose(row_inner)[:, :, None])
    score_low = score_grad.astype(jnp.bfloat16)
    query_grad = (
        jnp.einsum("hqk,khe->qhe", score_low, key_rows, preferred_element_type=jnp.float32)
        * softmax_scale
    ).astype(jnp.bfloat16)
    key_grad = (
        jnp.einsum("hqk,qhe->khe", score_low, queries, preferred_element_type=jnp.float32)
        * softmax_scale
    ).astype(jnp.bfloat16)
    value_grad = jnp.einsum(
        "hqk,qhe->khe", weights_low, grad_out, preferred_element_type=jnp.float32
    ).astype(jnp.bfloat16)
    return (attended, query_grad, key_grad, value_grad)


def attend_heads(queries, key_rows, value_rows, grad_out, shift_flags):
    total, heads, depth = queries.shape
    groups = total // GROUP

    def regroup(array):
        return shift_heads(array, shift_flags, -SHIFT).reshape(groups, GROUP, heads, depth)

    results = lax.map(
        group_block, (regroup(queries), regroup(key_rows), regroup(value_rows), regroup(grad_out))
    )
    return tuple(
        (
            shift_heads(output_part.reshape(total, heads, depth), shift_flags, SHIFT)
            for output_part in results
        )
    )


def body(
    normed_hidden_input,
    frozen_query_projection,
    frozen_key_projection,
    frozen_value_projection,
    cotangent,
    adapter_down_maps,
    adapter_up_maps,
    head_shift_mask,
):
    ctx_count = lax.axis_size("ctx")
    model_width = normed_hidden_input.shape[2]
    local_width = model_width // ctx_count
    local_heads = local_width // HEAD_DIM
    hidden_rows = normed_hidden_input[0]
    reduced_rank_rows = jnp.einsum(
        "vl,hlq->hvq", hidden_rows, adapter_down_maps, preferred_element_type=jnp.float32
    ).astype(jnp.bfloat16)
    frozen_stack = jnp.stack(
        [frozen_query_projection[0], frozen_key_projection[0], frozen_value_projection[0]]
    )
    grad_heads = lax.all_to_all(cotangent[0], "ctx", split_axis=1, concat_axis=0, tiled=True)
    local_flags = lax.dynamic_slice_in_dim(
        head_shift_mask, lax.axis_index("ctx") * local_heads, local_heads
    )
    adapter_update = jnp.einsum(
        "bsc,bci->bsi", reduced_rank_rows, adapter_up_maps, preferred_element_type=jnp.float32
    )
    projected_sequence = (frozen_stack.astype(jnp.float32) + adapter_scale * adapter_update).astype(
        jnp.bfloat16
    )
    projected_rows = lax.all_to_all(
        projected_sequence, "ctx", split_axis=2, concat_axis=1, tiled=True
    )
    seq_total = projected_rows.shape[1]
    head_view = projected_rows.reshape(3, seq_total, local_heads, HEAD_DIM)
    grad_view = grad_heads.reshape(seq_total, local_heads, HEAD_DIM)
    attended, query_grad, key_grad, value_grad = attend_heads(
        head_view[0], head_view[1], head_view[2], grad_view, local_flags
    )
    context = lax.all_to_all(
        attended.reshape(seq_total, local_width), "ctx", split_axis=0, concat_axis=1, tiled=True
    )
    grad_stack = jnp.stack([query_grad, key_grad, value_grad]).reshape(3, seq_total, local_width)
    token_gradient = lax.all_to_all(grad_stack, "ctx", split_axis=1, concat_axis=2, tiled=True)
    up_contribution = adapter_scale * jnp.einsum(
        "xvq,xvh->xqh", reduced_rank_rows, token_gradient, preferred_element_type=jnp.float32
    )
    backward_rank_rows = jnp.einsum(
        "efu,eau->efa", token_gradient, adapter_up_maps, preferred_element_type=jnp.float32
    ).astype(jnp.bfloat16)
    down_contribution = adapter_scale * jnp.einsum(
        "ow,noi->nwi", hidden_rows, backward_rank_rows, preferred_element_type=jnp.float32
    )
    grad_down, grad_up = lax.psum((down_contribution, up_contribution), ("dp", "ctx"))
    return (context[None], grad_down, grad_up)


def solution(mesh):
    placed = (
        P("dp", "ctx", None),
        P("dp", "ctx", None),
        P("dp", "ctx", None),
        P("dp", "ctx", None),
        P("dp", "ctx", None),
        P(),
        P(),
        P(),
    )
    return jax.shard_map(
        body,
        mesh=mesh,
        in_specs=placed,
        out_specs=(P("dp", "ctx", None), P(), P()),
        check_vma=False,
    )
```

profile of v0, /device:TPU:2, one launch (start us, length us, event | category | flops | bytes accessed | tf_op | source)
XLA Modules:
  0.0 671.0 jit_solution(5635035876560614335)
XLA Ops:
  7.2 2.4 copy.90
  9.6 11.6 %all-to-all-start.1 = ((bf16[128,32,128]{0,2,1:T(8,128)(2,1)}), bf16[128,32,128]{0,2,1:T(8,128)(2,1)S(1)}, u32[]{:S(2)}, u32[]{:S(2)}) async-start(bf16[128,32,128]{0,2,1:T(8,128)(2,1)} %bitcast.39), calls=%async_computation.1 | async-start | bytes 2097152 | tf_op jit(solution)/shard_map/all_to_all | solution.py:95
  22.3 3.7 add_convert_fusion
  26.1 7.1 %copy.79 = bf16[3,128,4096]{1,0,2:T(4,128)(2,1)} copy(bf16[3,128,4096]{2,1,0:T(8,128)(2,1)} %add_convert_fusion) | data formatting | bytes 6291456 | tf_op jit(solution)/shard_map/convert_element_type | solution.py:102
  33.2 16.1 %all-to-all-done.1 = bf16[128,32,128]{0,2,1:T(8,128)(2,1)S(1)} async-done(((bf16[128,32,128]{0,2,1:T(8,128)(2,1)}), bf16[128,32,128]{0,2,1:T(8,128)(2,1)S(1)}, u32[]{:S(2)}, u32[]{:S(2)}) %all-to-all-start.1) | async-done | bytes 1048608 | tf_op jit(solution)/shard_map/all_to_all | solution.py:95
  49.3 5.6 all-to-all-start
  58.0 1.6 copy.91
  59.8 1.2 broadcast_select_fusion
  61.0 85.8 %all-to-all-done = bf16[3,128,4096]{1,0,2:T(4,128)(2,1)} async-done(((bf16[3,128,4096]{1,0,2:T(4,128)(2,1)}), bf16[3,128,4096]{1,0,2:T(4,128)(2,1)}, u32[]{:S(2)}, u32[]{:S(2)}) %all-to-all-start) | async-done | bytes 3145760 | tf_op jit(solution)/shard_map/all_to_all | solution.py:105
  146.8 2.6 copy.80
  149.5 1.6 fusion.47
  151.7 1.7 fusion.46
  153.4 1.3 copy.87
  155.4 2.2 copy.84
  157.8 1.6 copy.86
  159.4 2.3 copy.81
  162.7 2.3 copy.83
  165.0 1.3 pad_maximum_fusion.2
  166.3 1.1 select_bitcast_fusion
  170.1 81.5 %while.16 = (s32[]{:T(128)}, bf16[4,1024,1,128]{3,1,0,2:T(8,128)(2,1)}, bf16[4,1024,1,128]{3,1,0,2:T(8,128)(2,1)}, bf16[4,1024,1,128]{3,1,0,2:T(8,128)(2,1)}, bf...) while((s32[]{:T(128)}, ...), condition=%wide.region_4.5_spmd, body=%wide.region_0.4_spmd.sunk | while | flops 1642329088 | bytes 69517472 | solution.py:63
  170.1 1.7 fusion.78
  172.3 1.2 constant_dynamic-slice_fusion.2
  175.7 3.9 fusion.80
  179.6 1.9 multiply_convert_fusion.2
  181.5 2.5 fusion.83
  185.1 1.8 constant_dynamic-update-slice_fusion.7
  186.9 1.4 fusion.81
  190.4 1.7 fusion.78
  192.7 1.2 constant_dynamic-slice_fusion.2
  196.0 3.9 fusion.80
  199.9 1.9 multiply_convert_fusion.2
  201.8 2.5 fusion.83
  205.4 1.8 constant_dynamic-update-slice_fusion.7
  207.2 1.4 fusion.81
  208.8 1.1 copy.141
  210.8 1.7 fusion.78
  213.0 1.2 constant_dynamic-slice_fusion.2
  216.4 3.9 fusion.80
  220.3 1.9 multiply_convert_fusion.2
  222.2 2.5 fusion.83
  225.8 1.8 constant_dynamic-update-slice_fusion.7
  227.6 1.4 fusion.81
  231.1 1.7 fusion.78
  233.4 1.2 constant_dynamic-slice_fusion.2
  236.8 3.9 fusion.80
  240.6 1.9 multiply_convert_fusion.2
  242.5 2.5 fusion.83
  246.2 1.8 constant_dynamic-update-slice_fusion.7
  248.0 1.4 fusion.81
  251.5 1.3 slice_bitcast_fusion.1
  253.9 1.2 slice_bitcast_fusion.2
  257.6 20.8 %copy.107 = bf16[3,4096,128]{2,0,1:T(4,128)(2,1)} copy(bf16[3,4096,128]{2,1,0:T(8,128)(2,1)S(1)} %maximum_bitcast_fusion) | data formatting | bytes 6291456 | tf_op jit(solution)/shard_map/reshape | solution.py:117
  278.4 8.5 %all-to-all-start.3 = ((bf16[3,4096,128]{2,0,1:T(4,128)(2,1)}), bf16[3,4096,128]{2,0,1:T(4,128)(2,1)}, u32[]{:S(2)}, u32[]{:S(2)}) async-start(bf16[3,4096,128]{2,0,1:T(4,128)(2,1)} %copy.107), calls=%async_computation.3 | async-start | bytes 8388608 | tf_op jit(solution)/shard_map/all_to_all | solution.py:118
  288.2 91.0 %all-to-all-done.3 = bf16[3,4096,128]{2,0,1:T(4,128)(2,1)} async-done(((bf16[3,4096,128]{2,0,1:T(4,128)(2,1)}), bf16[3,4096,128]{2,0,1:T(4,128)(2,1)}, u32[]{:S(2)}, u32[]{:S(2)}) %all-to-all-start.3) | async-done | bytes 3145760 | tf_op jit(solution)/shard_map/all_to_all | solution.py:118
  379.1 7.5 %all-to-all-start.2 = ((bf16[32,128,128]{2,1,0:T(8,128)(2,1)}), bf16[32,128,128]{2,1,0:T(8,128)(2,1)S(1)}, u32[]{:S(2)}, u32[]{:S(2)}) async-start(bf16[32,128,128]{2,1,0:T(8,128)(2,1)} %broadcast_select_fusion.1), calls=%async_computation.2 | async-start | bytes 2097152 | tf_op jit(solution)/shard_map/all_to_all | solution.py:114
  386.7 2.7 copy.108
  389.4 1.6 copy-done.3
  391.0 1.4 convolution_multiply_fusion.2
  392.4 4.2 fusion.33
  396.7 16.3 %all-to-all-done.2 = bf16[32,128,128]{2,1,0:T(8,128)(2,1)S(1)} async-done(((bf16[32,128,128]{2,1,0:T(8,128)(2,1)}), bf16[32,128,128]{2,1,0:T(8,128)(2,1)S(1)}, u32[]{:S(2)}, u32[]{:S(2)}) %all-to-all-start.2) | async-done | bytes 1048608 | tf_op jit(solution)/shard_map/all_to_all | solution.py:114
  413.6 1.3 copy.110
  414.9 245.1 %all-reduce.3.cloned.1.call-done = (f32[3,4096,16]{1,2,0:T(8,128)}, f32[3,16,4096]{2,1,0:T(8,128)}) async-done(((f32[3,4096,16]{1,2,0:T(8,128)}, f32[3,16,4096]{2,1,0:T(8,128)}), (f32[3,4096,16]{1,2,0:T(8,128)}, f32[3,16,4096]{2,1,0:T(8,128)})) %all-reduce.3.cloned.1.call-update) | async-done | bytes 1572880 | tf_op jit(solution)/shard_map/psum | solution.py:128
  660.1 2.1 copy.167
  662.1 2.1 copy.168
  (110 shorter events, 36.8 us)
Async XLA Ops:
  7.2 14.1 %copy-start = (bf16[1,128,4096]{2,1,0:T(8,128)(2,1)S(1)}, bf16[1,128,4096]{2,1,0:T(8,128)(2,1)}, u32[]{:S(2)}) copy-start(bf16[1,128,4096]{2,1,0:T(8,128)(2,1)} %param.10) | copy-start | bytes 3145732
  7.2 14.0 %copy-start.11 = (bf16[3,4096,16]{1,2,0:T(8,128)(2,1)S(1)}, bf16[3,4096,16]{1,2,0:T(8,128)(2,1)}, u32[]{:S(2)}) copy-start(bf16[3,4096,16]{1,2,0:T(8,128)(2,1)} %param.15) | copy-start | bytes 1179652
  7.2 15.1 %copy-start.12 = (bf16[3,16,4096]{2,1,0:T(8,128)(2,1)S(1)}, bf16[3,16,4096]{2,1,0:T(8,128)(2,1)}, u32[]{:S(2)}) copy-start(bf16[3,16,4096]{2,1,0:T(8,128)(2,1)} %param.16) | copy-start | bytes 1179652
  9.6 39.7 %all-to-all-start.1 = ((bf16[128,32,128]{0,2,1:T(8,128)(2,1)}), bf16[128,32,128]{0,2,1:T(8,128)(2,1)S(1)}, u32[]{:S(2)}, u32[]{:S(2)}) async-start(bf16[128,32,128]{0,2,1:T(8,128)(2,1)} %bitcast.39), calls=%async_computation.1 | async-start | bytes 2097152 | tf_op jit(solution)/shard_map/all_to_all | solution.py:95
  21.7 0.6 copy-start.14
  33.2 21.8 %copy-start.16 = (s32[32]{0:T(128)S(1)}, s32[32]{0:T(128)}, u32[]{:S(2)}) copy-start(s32[32]{0:T(128)} %param.17) | copy-start | bytes 388
  49.3 97.5 %all-to-all-start = ((bf16[3,128,4096]{1,0,2:T(4,128)(2,1)}), bf16[3,128,4096]{1,0,2:T(4,128)(2,1)}, u32[]{:S(2)}, u32[]{:S(2)}) async-start(bf16[3,128,4096]{1,0,2:T(4,128)(2,1)} %copy.79), calls=%async_computation | async-start | bytes 8388608 | tf_op jit(solution)/shard_map/all_to_all | solution.py:105
  165.0 2.5 copy-start.9
  166.3 2.3 copy-start.10
  167.5 1.5 copy-start.8
  171.8 2.0 copy-start.1
  175.7 3.9 copy-start.2
  192.2 2.0 copy-start.1
  196.0 3.9 copy-start.2
  212.5 2.0 copy-start.1
  216.4 3.9 copy-start.2
  232.9 2.0 copy-start.1
  236.7 3.9 copy-start.2
  251.5 4.6 copy-start.7
  252.9 3.7 copy-start.4
  252.9 3.7 copy-start.5
  278.4 8.5 %copy-start.6 = (bf16[4,1024,1,128]{3,1,0,2:T(8,128)(2,1)S(1)}, bf16[4,1024,1,128]{3,1,0,2:T(8,128)(2,1)}, u32[]{:S(2)}) copy-start(bf16[4,1024,1,128]{3,1,0,2:T(8,128)(2,1)} %get-tuple-element.53) | copy-start | bytes 3145732
  278.4 100.7 %all-to-all-start.3 = ((bf16[3,4096,128]{2,0,1:T(4,128)(2,1)}), bf16[3,4096,128]{2,0,1:T(4,128)(2,1)}, u32[]{:S(2)}, u32[]{:S(2)}) async-start(bf16[3,4096,128]{2,0,1:T(4,128)(2,1)} %copy.107), calls=%async_computation.3 | async-start | bytes 8388608 | tf_op jit(solution)/shard_map/all_to_all | solution.py:118
  379.1 33.8 %all-to-all-start.2 = ((bf16[32,128,128]{2,1,0:T(8,128)(2,1)}), bf16[32,128,128]{2,1,0:T(8,128)(2,1)S(1)}, u32[]{:S(2)}, u32[]{:S(2)}) async-start(bf16[32,128,128]{2,1,0:T(8,128)(2,1)} %broadcast_select_fusion.1), calls=%async_computation.2 | async-start | bytes 2097152 | tf_op jit(solution)/shard_map/all_to_all | solution.py:114
  386.6 4.4 copy-start.15
  386.6 5.8 copy-start.13
  386.7 273.4 %all-reduce.3.cloned.1.call-start = ((), (), s32[]{:S(2)}) async-start(), calls=%async_computation.4 | async-start | bytes 3145728 | tf_op jit(solution)/shard_map/psum | solution.py:128
  389.4 1.6 copy-start.3
Sparse Core Ops, SparseCore 0:
  396.8 263.2 all-reduce.2
where the time goes:
time: 673 us; the launch traced here: 671 us
  waiting for transfers between devices  454 us (67%)
  local copies, waits for them, and re-layouts  98.2 us (15%)
  matrix products  59.2 us (9%)
  starting transfers between devices  33.3 us (5%)
  between operations  15.1 us (2%)
  other arithmetic  10.7 us (2%)
    psum x1, waiting for transfers between devices, body(): lax.psum((down_contribution, up_contribution), ('dp', 'ctx'))  245 us
    all_to_all x1, waiting for transfers between devices, body(): lax.all_to_all(grad_stack, 'ctx', split_axis=1, concat_axis=2, tiled=True)  91 us
    all_to_all x1, waiting for transfers between devices, body(): lax.all_to_all(projected_sequence, 'ctx', split_axis=2, concat_axis=1, ti...  85.8 us
    dynamic_update_slice x24, local copies, waits for them, and re-layouts, attend_heads(): lax.map(group_block, (regroup(queries), regroup(key_rows), regroup(value_...  23.5 us
    reshape x1, local copies, waits for them, and re-layouts, body(): jnp.stack([query_grad, key_grad, value_grad])  20.8 us
    all_to_all x1, waiting for transfers between devices, body(): lax.all_to_all(attended.reshape(seq_total, local_width), 'ctx', split_axi...  16.3 us
    all_to_all x1, waiting for transfers between devices, body(): lax.all_to_all(cotangent[0], 'ctx', split_axis=1, concat_axis=0, tiled=True)  16.1 us
    dot_general x4, matrix products, group_block(): jnp.einsum('hqk,khe->qhe', weights_low, value_rows, preferred_element_typ...  15.5 us
  transfers between devices with their start and end apart: 5, of which 5 were waited for; matrix products, arithmetic and copies ran while one was open for 4% of the time, Pallas kernels for 0%

commit v1 on v0

--- a/solution.py
+++ b/solution.py
@@ -111,8 +111,16 @@
     attended, query_grad, key_grad, value_grad = attend_heads(
         head_view[0], head_view[1], head_view[2], grad_view, local_flags
     )
-    context = lax.all_to_all(
-        attended.reshape(seq_total, local_width), "ctx", split_axis=0, concat_axis=1, tiled=True
+    context = jnp.concatenate(
+        lax.all_to_all(
+            jnp.stack(
+                jnp.split(attended.reshape(seq_total, local_width), lax.axis_size("ctx"), axis=0)
+            ),
+            "ctx",
+            0,
+            0,
+        ),
+        axis=1,
     )
     grad_stack = jnp.stack([query_grad, key_grad, value_grad]).reshape(3, seq_total, local_width)
     token_gradient = lax.all_to_all(grad_stack, "ctx", split_axis=1, concat_axis=2, tiled=True)

time: 673 us -> 673 us (level)
  local copies, waits for them, and re-layouts: 98.2 us -> 118 us
  waiting for transfers between devices: 454 us -> 435 us
    unnamed x34 -> x65, local copies, waits for them, and re-layouts: 10.3 us -> 29.5 us
    all_to_all x1, waiting for transfers between devices: 91 us -> 72.1 us  [body(): lax.all_to_all(grad_stack, 'ctx', split_axis=1, concat_axis=2, tiled=True)]
  transfers between devices with their start and end apart: 5 -> 5, of which waited for: 5 -> 5; matrix products, arithmetic and copies ran while one was open for 4% -> 7% of each run, Pallas kernels for 0% -> 0%
where the time goes in v1:
time: 673 us; the launch traced here: 671 us
  waiting for transfers between devices  435 us (65%)
  local copies, waits for them, and re-layouts  118 us (18%)
  matrix products  59.2 us (9%)
  starting transfers between devices  33.1 us (5%)
  between operations  15.1 us (2%)
  other arithmetic  9.89 us (1%)
    psum x1, waiting for transfers between devices, body(): lax.psum((down_contribution, up_contribution), ('dp', 'ctx'))  245 us
    all_to_all x1, waiting for transfers between devices, body(): lax.all_to_all(projected_sequence, 'ctx', split_axis=2, concat_axis=1, ti...  85.8 us
    all_to_all x1, waiting for transfers between devices, body(): lax.all_to_all(grad_stack, 'ctx', split_axis=1, concat_axis=2, tiled=True)  72.1 us
    unnamed x65, local copies, waits for them, and re-layouts  29.5 us
    dynamic_update_slice x24, local copies, waits for them, and re-layouts, attend_heads(): lax.map(group_block, (regroup(queries), regroup(key_rows), regroup(value_...  23.5 us
    reshape x1, local copies, waits for them, and re-layouts, body(): jnp.stack([query_grad, key_grad, value_grad])  20.8 us
    all_to_all x1, waiting for transfers between devices, body(): lax.all_to_all(jnp.stack(jnp.split(attended.reshape(seq_total, local_widt...  16.3 us
    all_to_all x1, waiting for transfers between devices, body(): lax.all_to_all(cotangent[0], 'ctx', split_axis=1, concat_axis=0, tiled=True)  16.1 us
  transfers between devices with their start and end apart: 5, of which 5 were waited for; matrix products, arithmetic and copies ran while one was open for 7% of the time, Pallas kernels for 0%

profile of v1, /device:TPU:2, one launch (start us, length us, event | category | flops | bytes accessed | tf_op | source)
XLA Modules:
  0.0 671.1 jit_solution(4737546883255023125)
XLA Ops:
  7.2 2.4 copy.117
  9.6 11.6 %all-to-all-start.1 = ((bf16[128,32,128]{0,2,1:T(8,128)(2,1)}), bf16[128,32,128]{0,2,1:T(8,128)(2,1)S(1)}, u32[]{:S(2)}, u32[]{:S(2)}) async-start(bf16[128,32,128]{0,2,1:T(8,128)(2,1)} %bitcast.39), calls=%async_computation.1 | async-start | bytes 2097152 | tf_op jit(solution)/shard_map/all_to_all | solution.py:95
  22.3 3.7 add_convert_fusion
  26.1 7.1 %copy.106 = bf16[3,128,4096]{1,0,2:T(4,128)(2,1)} copy(bf16[3,128,4096]{2,1,0:T(8,128)(2,1)} %add_convert_fusion) | data formatting | bytes 6291456 | tf_op jit(solution)/shard_map/convert_element_type | solution.py:102
  33.2 16.1 %all-to-all-done.1 = bf16[128,32,128]{0,2,1:T(8,128)(2,1)S(1)} async-done(((bf16[128,32,128]{0,2,1:T(8,128)(2,1)}), bf16[128,32,128]{0,2,1:T(8,128)(2,1)S(1)}, u32[]{:S(2)}, u32[]{:S(2)}) %all-to-all-start.1) | async-done | bytes 1048608 | tf_op jit(solution)/shard_map/all_to_all | solution.py:95
  49.3 5.6 all-to-all-start
  58.0 1.6 copy.118
  59.8 1.2 broadcast_select_fusion
  61.0 85.8 %all-to-all-done = bf16[3,128,4096]{1,0,2:T(4,128)(2,1)} async-done(((bf16[3,128,4096]{1,0,2:T(4,128)(2,1)}), bf16[3,128,4096]{1,0,2:T(4,128)(2,1)}, u32[]{:S(2)}, u32[]{:S(2)}) %all-to-all-start) | async-done | bytes 3145760 | tf_op jit(solution)/shard_map/all_to_all | solution.py:105
  146.8 2.6 copy.107
  149.5 1.6 fusion.47
  151.7 1.7 fusion.46
  153.4 1.3 copy.114
  155.4 2.2 copy.111
  157.8 1.6 copy.113
  159.4 2.3 copy.108
  162.7 2.3 copy.110
  165.0 1.3 pad_maximum_fusion.2
  166.3 1.1 select_bitcast_fusion
  170.1 81.5 %while.16 = (s32[]{:T(128)}, bf16[4,1024,1,128]{3,1,0,2:T(8,128)(2,1)}, bf16[4,1024,1,128]{3,1,0,2:T(8,128)(2,1)}, bf16[4,1024,1,128]{3,1,0,2:T(8,128)(2,1)}, bf...) while((s32[]{:T(128)}, ...), condition=%wide.region_4.5_spmd, body=%wide.region_0.4_spmd.sunk | while | flops 1642329088 | bytes 69517472 | solution.py:63
  170.1 1.7 fusion.78
  172.3 1.2 constant_dynamic-slice_fusion.2
  175.7 3.9 fusion.80
  179.6 1.9 multiply_convert_fusion.2
  181.5 2.5 fusion.83
  185.1 1.8 constant_dynamic-update-slice_fusion.39
  186.9 1.4 fusion.81
  190.4 1.7 fusion.78
  192.7 1.2 constant_dynamic-slice_fusion.2
  196.0 3.9 fusion.80
  199.9 1.9 multiply_convert_fusion.2
  201.8 2.5 fusion.83
  205.4 1.8 constant_dynamic-update-slice_fusion.39
  207.2 1.4 fusion.81
  208.8 1.1 copy.167
  210.8 1.7 fusion.78
  213.0 1.2 constant_dynamic-slice_fusion.2
  216.4 3.9 fusion.80
  220.3 1.9 multiply_convert_fusion.2
  222.2 2.5 fusion.83
  225.8 1.8 constant_dynamic-update-slice_fusion.39
  227.6 1.4 fusion.81
  231.1 1.7 fusion.78
  233.4 1.2 constant_dynamic-slice_fusion.2
  236.8 3.9 fusion.80
  240.6 1.9 multiply_convert_fusion.2
  242.5 2.5 fusion.83
  246.2 1.8 constant_dynamic-update-slice_fusion.39
  248.0 1.4 fusion.81
  251.5 1.4 slice_bitcast_fusion.1
  253.8 1.2 slice_bitcast_fusion.2
  257.8 20.8 %copy.133 = bf16[3,4096,128]{2,0,1:T(4,128)(2,1)} copy(bf16[3,4096,128]{2,1,0:T(8,128)(2,1)S(1)} %maximum_bitcast_fusion) | data formatting | bytes 6291456 | tf_op jit(solution)/shard_map/reshape | solution.py:125
  278.5 8.4 %all-to-all-start.3 = ((bf16[3,4096,128]{2,0,1:T(4,128)(2,1)}), bf16[3,4096,128]{2,0,1:T(4,128)(2,1)}, u32[]{:S(2)}, u32[]{:S(2)}) async-start(bf16[3,4096,128]{2,0,1:T(4,128)(2,1)} %copy.133), calls=%async_computation.3 | async-start | bytes 8388608 | tf_op jit(solution)/shard_map/all_to_all | solution.py:126
  307.0 72.1 %all-to-all-done.3 = bf16[3,4096,128]{2,0,1:T(4,128)(2,1)} async-done(((bf16[3,4096,128]{2,0,1:T(4,128)(2,1)}), bf16[3,4096,128]{2,0,1:T(4,128)(2,1)}, u32[]{:S(2)}, u32[]{:S(2)}) %all-to-all-start.3) | async-done | bytes 3145760 | tf_op jit(solution)/shard_map/all_to_all | solution.py:126
  379.2 7.5 %all-to-all-start.2 = ((bf16[32,128,128]{2,1,0:T(8,128)(2,1)}), bf16[32,128,128]{2,1,0:T(8,128)(2,1)S(1)}, u32[]{:S(2)}, u32[]{:S(2)}) async-start(bf16[32,128,128]{2,1,0:T(8,128)(2,1)} %constant_dynamic-update-slice_fusion.4), calls=%async_computation.2 | async-start | bytes 2097152 | tf_op jit(solution)/shard_map/all_to_all | solution.py:115
  386.7 2.7 copy.134
  389.4 1.6 copy-done.3
  391.1 1.4 convolution_multiply_fusion.2
  392.5 4.2 fusion.33
  396.7 16.3 %all-to-all-done.2 = bf16[32,128,128]{2,1,0:T(8,128)(2,1)S(1)} async-done(((bf16[32,128,128]{2,1,0:T(8,128)(2,1)}), bf16[32,128,128]{2,1,0:T(8,128)(2,1)S(1)}, u32[]{:S(2)}, u32[]{:S(2)}) %all-to-all-start.2) | async-done | bytes 1048608 | tf_op jit(solution)/shard_map/all_to_all | solution.py:115
  413.6 1.3 copy.136
  415.0 245.1 %all-reduce.3.cloned.1.call-done = (f32[3,4096,16]{1,2,0:T(8,128)}, f32[3,16,4096]{2,1,0:T(8,128)}) async-done(((f32[3,4096,16]{1,2,0:T(8,128)}, f32[3,16,4096]{2,1,0:T(8,128)}), (f32[3,4096,16]{1,2,0:T(8,128)}, f32[3,16,4096]{2,1,0:T(8,128)})) %all-reduce.3.cloned.1.call-update) | async-done | bytes 1572880 | tf_op jit(solution)/shard_map/psum | solution.py:136
  660.1 2.1 copy.224
  662.2 2.1 copy.225
  (141 shorter events, 55.7 us)
Async XLA Ops:
  7.2 14.1 %copy-start = (bf16[1,128,4096]{2,1,0:T(8,128)(2,1)S(1)}, bf16[1,128,4096]{2,1,0:T(8,128)(2,1)}, u32[]{:S(2)}) copy-start(bf16[1,128,4096]{2,1,0:T(8,128)(2,1)} %param.10) | copy-start | bytes 3145732
  7.2 14.0 %copy-start.11 = (bf16[3,4096,16]{1,2,0:T(8,128)(2,1)S(1)}, bf16[3,4096,16]{1,2,0:T(8,128)(2,1)}, u32[]{:S(2)}) copy-start(bf16[3,4096,16]{1,2,0:T(8,128)(2,1)} %param.15) | copy-start | bytes 1179652
  7.2 15.1 %copy-start.12 = (bf16[3,16,4096]{2,1,0:T(8,128)(2,1)S(1)}, bf16[3,16,4096]{2,1,0:T(8,128)(2,1)}, u32[]{:S(2)}) copy-start(bf16[3,16,4096]{2,1,0:T(8,128)(2,1)} %param.16) | copy-start | bytes 1179652
  9.6 39.7 %all-to-all-start.1 = ((bf16[128,32,128]{0,2,1:T(8,128)(2,1)}), bf16[128,32,128]{0,2,1:T(8,128)(2,1)S(1)}, u32[]{:S(2)}, u32[]{:S(2)}) async-start(bf16[128,32,128]{0,2,1:T(8,128)(2,1)} %bitcast.39), calls=%async_computation.1 | async-start | bytes 2097152 | tf_op jit(solution)/shard_map/all_to_all | solution.py:95
  21.7 0.6 copy-start.14
  33.2 21.8 %copy-start.16 = (s32[32]{0:T(128)S(1)}, s32[32]{0:T(128)}, u32[]{:S(2)}) copy-start(s32[32]{0:T(128)} %param.17) | copy-start | bytes 388
  49.3 97.5 %all-to-all-start = ((bf16[3,128,4096]{1,0,2:T(4,128)(2,1)}), bf16[3,128,4096]{1,0,2:T(4,128)(2,1)}, u32[]{:S(2)}, u32[]{:S(2)}) async-start(bf16[3,128,4096]{1,0,2:T(4,128)(2,1)} %copy.106), calls=%async_computation | async-start | bytes 8388608 | tf_op jit(solution)/shard_map/all_to_all | solution.py:105
  165.0 2.5 copy-start.9
  166.3 2.3 copy-start.10
  167.5 1.5 copy-start.8
  171.8 2.0 copy-start.1
  175.7 3.9 copy-start.2
  192.2 2.0 copy-start.1
  196.0 3.9 copy-start.2
  212.5 2.0 copy-start.1
  216.4 3.9 copy-start.2
  232.9 2.0 copy-start.1
  236.7 3.9 copy-start.2
  251.5 4.6 copy-start.7
  251.5 4.7 copy-start.6
  255.1 1.6 copy-start.4
  255.1 1.6 copy-start.5
  278.5 100.6 %all-to-all-start.3 = ((bf16[3,4096,128]{2,0,1:T(4,128)(2,1)}), bf16[3,4096,128]{2,0,1:T(4,128)(2,1)}, u32[]{:S(2)}, u32[]{:S(2)}) async-start(bf16[3,4096,128]{2,0,1:T(4,128)(2,1)} %copy.133), calls=%async_computation.3 | async-start | bytes 8388608 | tf_op jit(solution)/shard_map/all_to_all | solution.py:126
  379.2 33.8 %all-to-all-start.2 = ((bf16[32,128,128]{2,1,0:T(8,128)(2,1)}), bf16[32,128,128]{2,1,0:T(8,128)(2,1)S(1)}, u32[]{:S(2)}, u32[]{:S(2)}) async-start(bf16[32,128,128]{2,1,0:T(8,128)(2,1)} %constant_dynamic-update-slice_fusion.4), calls=%async_computation.2 | async-start | bytes 2097152 | tf_op jit(solution)/shard_map/all_to_all | solution.py:115
  386.7 4.4 copy-start.15
  386.7 5.8 copy-start.13
  386.7 273.4 %all-reduce.3.cloned.1.call-start = ((), (), s32[]{:S(2)}) async-start(), calls=%async_computation.4 | async-start | bytes 3145728 | tf_op jit(solution)/shard_map/psum | solution.py:136
  389.4 1.6 copy-start.3
Sparse Core Ops, SparseCore 0:
  396.8 263.2 all-reduce.2
